TPU v7x, 1024 devices: a whole 8x8x8 slice. The times are simulated.
1024 devices in a mesh: ctx: 64 (over x, z_lo, core), tp: 8 (over y), pp: 2 (over z_hi).
Axes of the slice: x: 8, y: 8, z: 8 (z_hi: 2, z_lo: 4; z = z_hi * 4 + z_lo), core: 2. Of those that a mesh axis runs over, the one named last changes fastest.
Arguments:
- queries: bfloat16 [2, 8192, 8192], P('pp', 'ctx', 'tp'), may hold values from -6 to 6
- key_feats: bfloat16 [2, 8192, 8192], P('pp', 'ctx', 'tp'), may hold values from -6 to 6
- value_feats: bfloat16 [2, 8192, 8192], P('pp', 'ctx', 'tp'), may hold values from -6 to 6
- cotangent: bfloat16 [2, 8192, 8192], P('pp', 'ctx', 'tp'), may hold values from -70 to 70
- filters: float32 [2, 512, 128], P('pp', 'tp'), may hold values from -0.5 to 0.5
Outputs:
- grad_queries: bfloat16 [2, 8192, 8192], P('pp', 'ctx', 'tp')
- grad_keys: bfloat16 [2, 8192, 8192], P('pp', 'ctx', 'tp')
- handed: bfloat16 [2, 8192, 8192], P('pp', 'ctx', 'tp')
- grad_filters: float32 [2, 512, 128], P('pp', 'tp')
All inputs are finite; a program needn't handle non-finite values.
Results may differ from a plain program's by a relative error of at most 0.0058.
Values may be sent and summed in bfloat16 or wider, within the bound.
No kernel may reach another device: no remote copies, remote signals or barrier semaphores. Data moves between devices by JAX's collectives and lax.ppermute only.
A program may use at most 64 MiB of HBM per device.

v0:
```python
import math

import jax
import jax.numpy as jnp
from jax import lax
from jax.sharding import PartitionSpec as P

TAPS = 128
GROUP = 16
GROUPS = 512


BLOCK_ROWS = 64


def from_behind(block, axis, distance):
    devices = range(lax.axis_size(axis))
    route = [(i - distance, i) for i in devices if i - distance in devices]
    return lax.ppermute(block, axis, route)


def build_kernel(taps_rows, row_count):
    groups_here = taps_rows.shape[0]
    padded = jnp.concatenate(
        [taps_rows, jnp.zeros((groups_here, row_count), taps_rows.dtype)], axis=1
    )
    tiled = jnp.tile(padded, (1, row_count))
    span = row_count + TAPS - 1
    return tiled[:, : row_count * span].reshape(groups_here, row_count, span)


def apply_kernel(kernel, window):
    groups_here, row_count, span = kernel.shape
    pieces = window.reshape(span, groups_here, GROUP)
    result = jnp.einsum("gts,sgc->tgc", kernel, pieces, preferred_element_type=jnp.float32)
    return result.reshape(row_count, groups_here * GROUP)


def apply_blocks(kernel, extended, first, count):
    span = BLOCK_ROWS + TAPS - 1
    parts = [
        apply_kernel(
            kernel,
            extended[
                (first + block_index) * BLOCK_ROWS : (first + block_index) * BLOCK_ROWS + span
            ],
        )
        for block_index in range(count)
    ]
    return jnp.concatenate(parts, axis=0)


def per_device(queries, key_feats, value_feats, cotangent, filters):
    query_rows = queries[0]
    key_rows = key_feats[0]
    value_rows = value_feats[0]
    cot_rows = cotangent[0]
    length = query_rows.shape[0]
    channels = query_rows.shape[1]
    halo_len = TAPS - 1
    block_rows = BLOCK_ROWS
    num_blocks = length // block_rows
    span = block_rows + halo_len
    tail_blocks = TAPS // block_rows
    last_start = length - TAPS
    taps_bf = filters[0].astype(jnp.bfloat16)
    groups_here = taps_bf.shape[0]
    kernel_fwd = build_kernel(taps_bf[:, ::-1], block_rows)
    kernel_back = build_kernel(taps_bf, block_rows)
    product = key_rows * value_rows
    weighted = cot_rows * query_rows
    incoming = from_behind(product[length - halo_len :], "ctx", 1)
    front_ext = jnp.concatenate([incoming, product], axis=0)
    mixed_rows = apply_blocks(kernel_fwd, front_ext, 0, num_blocks)
    grad_q = (cot_rows * mixed_rows).astype(jnp.bfloat16)
    zero_rim = jnp.zeros((halo_len, channels), jnp.bfloat16)
    early_ext = jnp.concatenate([weighted, zero_rim], axis=0)
    head_grads = []
    head_values = []
    head_count = num_blocks - tail_blocks
    following = from_behind(weighted[:halo_len], "ctx", -1)
    late_ext = jnp.concatenate([weighted, following], axis=0)
    last_block = apply_blocks(kernel_back, late_ext, 0, tail_blocks)
    tail_grad = (last_block * value_rows).astype(jnp.bfloat16)
    tail_values = (last_block * key_rows).astype(jnp.bfloat16)
    grad_k = jnp.concatenate(head_grads + [tail_grad], axis=0)
    boundary = jnp.concatenate(head_values + [tail_values], axis=0)
    handed = from_behind(boundary, "pp", -1)
    raw_grad = jnp.zeros((groups_here, TAPS), jnp.float32)
    for block_index in range(num_blocks):
        grad_block = weighted[block_index * block_rows : (block_index + 1) * block_rows].reshape(
            block_rows, groups_here, GROUP
        )
        window = front_ext[block_index * block_rows : block_index * block_rows + span].reshape(
            span, groups_here, GROUP
        )
        pairs = jnp.einsum("tgc,sgc->gts", grad_block, window, preferred_element_type=jnp.float32)
        flat = pairs.reshape(groups_here, block_rows * span)
        flat = jnp.concatenate([flat, jnp.zeros((groups_here, block_rows), jnp.float32)], axis=1)
        skewed = flat.reshape(groups_here, block_rows, span + 1).sum(axis=1)
        raw_grad = raw_grad + skewed[:, :TAPS][:, ::-1]
    clip_level = 0.25 * math.sqrt(lax.axis_size("pp") * GROUPS * TAPS)
    summed = lax.psum(raw_grad, "ctx")
    norm_sq = lax.psum(jnp.sum(summed * summed), ("tp", "pp"))
    factor = jnp.minimum(1.0, clip_level / (jnp.sqrt(norm_sq) + 1e-06))
    grad_f = summed * factor
    return (grad_q[None], grad_k[None], handed[None], grad_f[None])


def solution(mesh):
    placed = (
        P("pp", "ctx", "tp"),
        P("pp", "ctx", "tp"),
        P("pp", "ctx", "tp"),
        P("pp", "ctx", "tp"),
        P("pp", "tp", None),
    )
    return jax.shard_map(
        per_device,
        mesh=mesh,
        in_specs=placed,
        out_specs=(
            P("pp", "ctx", "tp"),
            P("pp", "ctx", "tp"),
            P("pp", "ctx", "tp"),
            P("pp", "tp", None),
        ),
        check_vma=False,
    )
```

profile of v0, /device:TPU:16, one launch (start us, length us, event | category | flops | bytes accessed | tf_op | source)
XLA Modules:
  0.0 442.1 jit_solution(14665410913752488840)
XLA Ops:
  1.8 1.8 collective-permute-start
  8.6 3.2 tile.21
  11.8 7.2 %reshape.85 = bf16[64,64,191]{2,1,0:T(8,128)(2,1)S(1)} reshape(bf16[64,12224]{1,0:T(8,128)(2,1)} %bitcast.51) | data formatting | bytes 3129344 | tf_op jit(solution)/shard_map/reshape | solution.py:29
  19.1 1.5 tile.8
  20.6 4.5 %tile.9 = bf16[64,12288]{1,0:T(8,128)(2,1)} reshape(bf16[64,64,192]{2,1,0:T(8,128)(2,1)} %tile.8) | data formatting | bytes 3145728 | tf_op jit(solution)/shard_map/tile | solution.py:27
  25.8 1.8 fusion.4
  27.8 3.6 fusion.10
  31.4 5.3 %reshape.90 = f32[64,12224]{1,0:T(8,128)} reshape(f32[64,64,191]{2,1,0:T(8,128)} %fusion.10) | data formatting | bytes 6258688 | tf_op jit(solution)/shard_map/reshape | solution.py:98
  36.7 3.8 concatenate.47
  40.6 5.2 %reshape.91 = f32[64,64,192]{2,1,0:T(8,128)} reshape(f32[64,12288]{1,0:T(8,128)} %concatenate.47) | data formatting | bytes 6291456 | tf_op jit(solution)/shard_map/reshape | solution.py:100
  45.8 2.8 reduce_sum.27
  49.8 3.6 fusion.11
  53.5 5.3 %reshape.93 = f32[64,12224]{1,0:T(8,128)} reshape(f32[64,64,191]{2,1,0:T(8,128)} %fusion.11) | data formatting | bytes 6258688 | tf_op jit(solution)/shard_map/reshape | solution.py:98
  58.8 3.8 concatenate.48
  62.6 5.2 %reshape.94 = f32[64,64,192]{2,1,0:T(8,128)} reshape(f32[64,12288]{1,0:T(8,128)} %concatenate.48) | data formatting | bytes 6291456 | tf_op jit(solution)/shard_map/reshape | solution.py:100
  67.8 2.8 reduce_sum.28
  70.6 277.5 %psum.14 = f32[64,128]{1,0:T(8,128)S(1)} all-reduce(f32[64,128]{1,0:T(8,128)S(1)} %add.18), channel_id=1, replica_groups=mesh['ctx'=64,'tp'=8,'pp'=2] {'ctx'}, use_global_device_ids=true, to_apply=%region_2.0 | all-reduce | flops 8192 | bytes 65536 | tf_op jit(solution)/shard_map/psum | solution.py:103
  348.8 8.0 %reshape.82 = bf16[64,64,191]{2,1,0:T(8,128)(2,1)} reshape(bf16[64,12224]{1,0:T(8,128)(2,1)} %bitcast.50) | data formatting | bytes 3129344 | tf_op jit(solution)/shard_map/reshape | solution.py:29
  356.8 58.5 %psum.15 = f32[]{:T(128)} all-reduce(f32[]{:T(128)} %multiply_reduce_fusion), channel_id=1, replica_groups=mesh['ctx'=64,'tp'=8,'pp'=2] {'tp','pp'}, use_global_device_ids=true, to_apply=%region_4.0 | all-reduce | flops 1 | bytes 8 | tf_op jit(solution)/shard_map/psum | solution.py:104
  416.0 3.2 fusion.6
  420.7 1.9 fusion.3
  425.3 1.7 fusion.9
  427.3 1.8 fusion.2
  433.3 8.1 %collective-permute-done.2 = bf16[128,1024]{1,0:T(8,128)(2,1)S(1)} collective-permute-done((bf16[128,1024]{1,0:T(8,128)(2,1)}, bf16[128,1024]{1,0:T(8,128)(2,1)S(1)}, u32[]{:S(2)}, u32[]{:S(2)}) %collective-permute-start.2) | collective-permute-done | bytes 262176 | tf_op jit(solution)/shard_map/ppermute | solution.py:19
  (60 shorter events, 18.4 us)
Async XLA Ops:
  0.6 7.8 %copy-start.10 = (f32[1,64,128]{2,1,0:T(8,128)S(1)}, f32[1,64,128]{2,1,0:T(8,128)}, u32[]{:S(2)}) copy-start(f32[1,64,128]{2,1,0:T(8,128)} %param.9) | copy-start | bytes 98308
  1.8 23.2 %collective-permute-start = (bf16[127,1024]{1,0:T(8,128)(2,1)S(1)}, bf16[127,1024]{1,0:T(8,128)(2,1)S(1)}, u32[]{:S(2)}, u32[]{:S(2)}) collective-permute-start(bf16[127,1024]{1,0:T(8,128)(2,1)S(1)} %slice_bitcast_fusion.1), channel_id=1, source_target_pairs={{0,16},{16,32},{32,48},{48,64},{64,80},{80,96},{96,112},{112,128},... | collective-permute-start | bytes 780296 | tf_op jit(solution)/shard_map/ppermute | solution.py:19
  5.4 415.3 %collective-permute-start.1 = (bf16[127,1024]{1,0:T(8,128)(2,1)}, bf16[127,1024]{1,0:T(8,128)(2,1)}, u32[]{:S(2)}, u32[]{:S(2)}) collective-permute-start(bf16[127,1024]{1,0:T(8,128)(2,1)} %slice_bitcast_fusion), channel_id=1, source_target_pairs={{16,0},{32,16},{48,32},{64,48},{80,64},{96,80},{112,96},{128,112},... | collective-permute-start | bytes 780296 | tf_op jit(solution)/shard_map/ppermute | solution.py:19
  25.1 0.7 copy-start.9
  348.2 71.0 %copy-start.7 = (f32[64,128]{1,0:T(8,128)}, f32[64,128]{1,0:T(8,128)S(1)}, u32[]{:S(2)}) copy-start(f32[64,128]{1,0:T(8,128)S(1)} %psum.14) | copy-start | bytes 98308
  416.0 3.2 copy-start
  422.8 1.6 copy-start.3
  425.3 1.9 copy-start.4
  427.0 3.7 copy-start.5
  427.0 4.5 %copy-start.8 = (f32[64,128]{1,0:T(8,128)S(1)}, f32[64,128]{1,0:T(8,128)}, u32[]{:S(2)}) copy-start(f32[64,128]{1,0:T(8,128)} %copy-done.7) | copy-start | bytes 98308
  427.0 5.1 %copy-start.1 = (f32[64,16,64]{2,1,0:T(8,128)S(1)}, f32[64,16,64]{2,1,0:T(8,128)}, u32[]{:S(2)}) copy-start(f32[64,16,64]{2,1,0:T(8,128)} %fusion.6) | copy-start | bytes 786436
  427.3 5.1 %copy-start.2 = (f32[64,16,64]{2,1,0:T(8,128)S(1)}, f32[64,16,64]{2,1,0:T(8,128)}, u32[]{:S(2)}) copy-start(f32[64,16,64]{2,1,0:T(8,128)} %fusion.7) | copy-start | bytes 786436
  429.0 12.4 %collective-permute-start.2 = (bf16[128,1024]{1,0:T(8,128)(2,1)}, bf16[128,1024]{1,0:T(8,128)(2,1)S(1)}, u32[]{:S(2)}, u32[]{:S(2)}) collective-permute-start(bf16[128,1024]{1,0:T(8,128)(2,1)} %fusion.2), channel_id=1, source_target_pairs={{1,0},{3,2},{5,4},{7,6},{9,8},{11,10},{13,12},{15,14},{17,16},{19,... | collective-permute-start | bytes 786440 | tf_op jit(solution)/shard_map/ppermute | solution.py:19
  430.3 2.2 copy-start.6
where the time goes:
time: 443 us; the launch traced here: 442 us
  blocking collectives  336 us (76%)
  local copies, waits for them, and re-layouts  61.8 us (14%)
  other arithmetic  15.9 us (4%)
  matrix products  14.3 us (3%)
  waiting for transfers between devices  8.1 us (2%)
    psum x1, blocking collectives, per_device(): summed = lax.psum(raw_grad, 'ctx')  278 us
    psum x1, blocking collectives, per_device(): norm_sq = lax.psum(jnp.sum(summed * summed), ('tp', 'pp'))  58.5 us
    reshape x2, local copies, waits for them, and re-layouts, build_kernel(): return tiled[:, :row_count * span].reshape(groups_here, row_count, span)  15.3 us
    reshape x2, local copies, waits for them, and re-layouts, per_device(): flat = pairs.reshape(groups_here, block_rows * span)  10.6 us
    reshape x2, local copies, waits for them, and re-layouts, per_device(): skewed = flat.reshape(groups_here, block_rows, span + 1).sum(axis=1)  10.4 us
    another operation x4, local copies, waits for them, and re-layouts, build_kernel(): tiled = jnp.tile(padded, (1, row_count))  9.28 us
  transfers between devices with their start and end apart: 3, of which 1 were waited for; matrix products, arithmetic and copies ran while one was open for 18% of the time, Pallas kernels for 0%

commit v1 on v0

v1 whole, which is shorter than its diff:
```python
import math

import jax
import jax.numpy as jnp
from jax import lax
from jax.experimental import pallas as pl
from jax.experimental.pallas import tpu as pltpu
from jax.sharding import Mesh, PartitionSpec as P


TAPS = 128
GROUP = 16
GROUPS = 512
LANES = 128
PER_BLOCK = LANES // GROUP

CTX = ("x", "zl", "core")
BF16 = jnp.bfloat16
F32 = jnp.float32


def flip_rows():
    row = lax.broadcasted_iota(jnp.int32, (LANES, LANES), 0)
    col = lax.broadcasted_iota(jnp.int32, (LANES, LANES), 1)
    return (row + col == LANES - 1).astype(F32).astype(BF16)


def dot(a, b):
    return jnp.dot(a, b, preferred_element_type=F32)


def products_kernel(k_ref, v_ref, c_ref, q_ref, p_ref, w_ref):
    flip = flip_rows()
    prod = k_ref[...] * v_ref[...]
    p_ref[...] = dot(flip, prod).astype(BF16)
    w_ref[...] = c_ref[...] * q_ref[...]


def filter_grad_kernel(w_ref, p_ref, hp_ref, raw_ref, stacked):
    row = lax.broadcasted_iota(jnp.int32, (LANES, LANES), 0)
    col = lax.broadcasted_iota(jnp.int32, (LANES, LANES), 1)
    own = row + col >= LANES - 1
    for block in range(w_ref.shape[1] // LANES):
        lanes = pl.ds(block * LANES, LANES)
        w = w_ref[:, lanes]
        for g in range(PER_BLOCK):
            stacked[pl.ds(g * LANES, LANES), :] = jnp.where(
                col // GROUP == g, w, jnp.zeros_like(w)
            )
        both = jnp.concatenate([p_ref[:, lanes], hp_ref[:, lanes]], axis=0)
        pairs = lax.dot_general(
            stacked[...], both, (((1,), (1,)), ((), ())), preferred_element_type=F32
        )
        for g in range(PER_BLOCK):
            part = pairs[g * LANES : (g + 1) * LANES]
            part = jnp.where(own, part[:, :LANES], part[:, LANES:])
            part = pltpu.roll(part, 1, 1, stride=1, stride_axis=0)
            raw_ref[pl.ds(block * PER_BLOCK + g, 1), :] = jnp.sum(part, axis=0, keepdims=True)


def mix_kernel(
    taps_ref, w_ref, hw_ref, p_ref, hp_ref, c_ref, k_ref, v_ref, gq_ref, gk_ref, dv_ref, stacked
):
    row = lax.broadcasted_iota(jnp.int32, (LANES, LANES), 0)
    col = lax.broadcasted_iota(jnp.int32, (LANES, LANES), 1)
    upper = col >= row
    flip = flip_rows()
    for block in range(w_ref.shape[1] // LANES):
        lanes = pl.ds(block * LANES, LANES)
        for g in range(PER_BLOCK):
            taps = taps_ref[pl.ds(block * PER_BLOCK + g, 1), :]
            taps = taps.astype(BF16).astype(F32)
            circ = pltpu.roll(
                jnp.broadcast_to(taps, (LANES, LANES)), 0, 1, stride=1, stride_axis=0
            )
            zero = jnp.zeros_like(circ)
            rows = pl.ds(g * LANES, LANES)
            stacked[rows, pl.ds(0, LANES)] = jnp.where(upper, circ, zero).astype(BF16)
            stacked[rows, pl.ds(LANES, LANES)] = jnp.where(upper, zero, circ).astype(BF16)
        data = jnp.concatenate(
            [
                jnp.concatenate([w_ref[:, lanes], p_ref[:, lanes]], axis=1),
                jnp.concatenate([hw_ref[:, lanes], hp_ref[:, lanes]], axis=1),
            ],
            axis=0,
        )
        out = dot(stacked[...], data)
        back = out[:LANES, :LANES]
        ahead = out[:LANES, LANES:]
        for g in range(1, PER_BLOCK):
            mine = col // GROUP == g
            back = jnp.where(mine, out[g * LANES : (g + 1) * LANES, :LANES], back)
            ahead = jnp.where(mine, out[g * LANES : (g + 1) * LANES, LANES:], ahead)
        gk_ref[:, lanes] = (back * v_ref[:, lanes].astype(F32)).astype(BF16)
        dv_ref[:, lanes] = (back * k_ref[:, lanes].astype(F32)).astype(BF16)
        cot = dot(flip, c_ref[:, lanes])
        gq_ref[:, lanes] = dot(flip, (cot * ahead).astype(BF16)).astype(BF16)


def exchange(rows, axes):
    return lax.all_to_all(rows, axes, 0, 0, tiled=True)


def per_device(queries, key_feats, value_feats, cotangent, filters):
    outs = block(queries[0], key_feats[0], value_feats[0], cotangent[0], filters[0])
    return tuple(out[None] for out in outs)


def block(q, k, v, c, filters):
    length, channels = q.shape
    groups_here = filters.shape[0]
    whole = jax.ShapeDtypeStruct((length, channels), BF16)
    size = length * channels * 2

    prod, weighted = pl.pallas_call(
        products_kernel,
        out_shape=(whole, whole),
        cost_estimate=pl.CostEstimate(
            flops=2 * LANES * length * channels, bytes_accessed=6 * size, transcendentals=0
        ),
    )(k, v, c, q)

    count = lax.axis_size(CTX)
    behind = lax.ppermute(prod, CTX, [(i, i + 1) for i in range(count - 1)])
    ahead = lax.ppermute(weighted, CTX, [(i + 1, i) for i in range(count - 1)])

    raw = pl.pallas_call(
        filter_grad_kernel,
        out_shape=jax.ShapeDtypeStruct((groups_here, TAPS), F32),
        scratch_shapes=[pltpu.VMEM((PER_BLOCK * LANES, LANES), BF16)],
        cost_estimate=pl.CostEstimate(
            flops=4 * groups_here * LANES**3, bytes_accessed=3 * size, transcendentals=0
        ),
    )(weighted, prod, behind)

    grad_q, grad_k, dvalues = pl.pallas_call(
        mix_kernel,
        out_shape=(whole, whole, whole),
        scratch_shapes=[pltpu.VMEM((PER_BLOCK * LANES, 2 * LANES), BF16)],
        cost_estimate=pl.CostEstimate(
            flops=8 * groups_here * LANES**3, bytes_accessed=10 * size, transcendentals=0
        ),
    )(filters, weighted, ahead, prod, behind, c, k, v)
    handed = lax.ppermute(dvalues, "pp", [(1, 0)])

    near = lax.axis_size(("zl", "core"))
    share = groups_here // near
    part = exchange(raw, ("zl", "core"))
    part = jnp.sum(part.reshape(near, share, TAPS), axis=0)
    wide = lax.axis_size("x")
    part = jnp.tile(part, (wide, 1))
    part = exchange(part, "x")
    part = jnp.sum(part.reshape(wide, share, TAPS), axis=0)
    square = jnp.sum(part * part, axis=0, keepdims=True)
    square = jnp.tile(square, (lax.axis_size("tp"), 1))
    square = exchange(square, "tp")
    square = jnp.sum(square, axis=0, keepdims=True)
    line = ("pp", "zl", "core")
    packed = jnp.concatenate([part, square], axis=0)
    packed = jnp.broadcast_to(packed[None], (lax.axis_size(line), share + 1, TAPS))
    packed = lax.all_to_all(packed, line, 0, 0)
    norm_sq = jnp.sum(packed[:, share])
    clip_level = 0.25 * math.sqrt(lax.axis_size("pp") * GROUPS * TAPS)
    factor = jnp.minimum(1.0, clip_level / (jnp.sqrt(norm_sq) + 1e-06))
    summed = lax.dynamic_slice_in_dim(packed, lax.axis_index("pp") * near, near, 0)
    grad_f = summed[:, :share].reshape(groups_here, TAPS) * factor
    return grad_q, grad_k, handed, grad_f


def solution(mesh):
    split = Mesh(
        mesh.devices.reshape(-1, 4, 2, mesh.shape["tp"], mesh.shape["pp"]),
        ("x", "zl", "core", "tp", "pp"),
    )
    acts = P("pp", CTX, "tp")
    taps = P("pp", "tp", None)
    return jax.shard_map(
        per_device,
        mesh=split,
        in_specs=(acts, acts, acts, acts, taps),
        out_specs=(acts, acts, acts, taps),
        check_vma=False,
    )
```

time: 443 us -> 98.8 us (0.22)
  the two profiles are of different devices: /device:TPU:16 before, /device:TPU:128 now
where the time goes in v1:
time: 98.8 us; the launch traced here: 98.3 us
  blocking collectives  28.8 us (29%)
  waiting for transfers between devices  28.3 us (29%)
  starting transfers between devices  24.3 us (25%)
  Pallas kernels  10.8 us (11%)
  local copies, waits for them, and re-layouts  3.39 us (3%)
  between operations  1.42 us (1%)
  other arithmetic  1.31 us (1%)
    all_to_all x2, blocking collectives, exchange(): return lax.all_to_all(rows, axes, 0, 0, tiled=True)  28.8 us
    ppermute x1, waiting for transfers between devices, block(): handed = lax.ppermute(dvalues, 'pp', [(1, 0)])  16.7 us
    all_to_all x1, starting transfers between devices, block(): packed = lax.all_to_all(packed, line, 0, 0)  12.6 us
    all_to_all x1, starting transfers between devices, exchange(): return lax.all_to_all(rows, axes, 0, 0, tiled=True)  6.13 us
    ppermute x1, waiting for transfers between devices, block(): behind = lax.ppermute(prod, CTX, [(i, i + 1) for i in range(count - 1)])  5.97 us
    all_to_all x1, waiting for transfers between devices, exchange(): return lax.all_to_all(rows, axes, 0, 0, tiled=True)  5.67 us
    pallas_call x1, Pallas kernels, block(): pl.pallas_call(mix_kernel, out_shape=(whole, whole, whole), scratch_shape...  5.35 us
    pallas_call x1, Pallas kernels, block(): pl.pallas_call(filter_grad_kernel, out_shape=jax.ShapeDtypeStruct((groups...  3.28 us
  transfers between devices with their start and end apart: 5, of which 3 were waited for; matrix products, arithmetic and copies ran while one was open for 2% of the time, Pallas kernels for 5%

profile of v1, /device:TPU:128, one launch (start us, length us, event | category | flops | bytes accessed | tf_op | source)
XLA Modules:
  0.0 98.3 jit_solution(8631125491993926776)
XLA Ops:
  0.6 2.2 %shard_map.84 = (bf16[128,1024]{1,0:T(8,128)(2,1)}, bf16[128,1024]{1,0:T(8,128)(2,1)}) custom-call(bf16[128,1024]{1,0:T(8,128)(2,1)} %bitcast.15, bf16[128,1024]{1,0:T(8,128)(2,1)} %bitcast.17, bf16[128,1024]{1,0:T(8,128)(2,1)} %bitcast.19, bf16[128,1024]{1,0:T(8,128)(2,1)} %bitcast.14), custom_call_target="tpu_custom_call" | custom-call | flops 33554432 | bytes 1572864 | tf_op jit(solution)/shard_map/pallas_call | solution.py:115
  2.8 1.9 %collective-permute-start.1 = (bf16[128,1024]{1,0:T(8,128)(2,1)}, bf16[128,1024]{1,0:T(8,128)(2,1)S(1)}, u32[]{:S(2)}, u32[]{:S(2)}) collective-permute-start(bf16[128,1024]{1,0:T(8,128)(2,1)} %get-tuple-element.10.p_ref), channel_id=1, source_target_pairs={{0,16},{16,32},{32,48},{48,64},{64,80},{80,96},{96,112},{112,128},... | collective-permute-start | bytes 786440 | tf_op jit(solution)/shard_map/ppermute | solution.py:124
  4.7 6.0 %collective-permute-done.1.hp_ref = bf16[128,1024]{1,0:T(8,128)(2,1)S(1)} collective-permute-done((bf16[128,1024]{1,0:T(8,128)(2,1)}, bf16[128,1024]{1,0:T(8,128)(2,1)S(1)}, u32[]{:S(2)}, u32[]{:S(2)}) %collective-permute-start.1) | collective-permute-done | bytes 262176 | tf_op jit(solution)/shard_map/ppermute | solution.py:124
  10.7 0.7 copy-done.1
  11.4 3.3 %shard_map.86 = f32[64,128]{1,0:T(8,128)} custom-call(bf16[128,1024]{1,0:T(8,128)(2,1)} %get-tuple-element.9.w_ref, bf16[128,1024]{1,0:T(8,128)(2,1)} %get-tuple-element.10.p_ref, bf16[128,1024]{1,0:T(8,128)(2,1)} %copy-done.1), custom_call_target="tpu_custom_call" | custom-call | flops 536870912 | bytes 786432 | tf_op jit(solution)/shard_map/pallas_call | solution.py:127
  14.7 13.7 %all_to_all.26 = f32[8,8,128]{2,1,0:T(8,128)S(1)} all-to-all(f32[8,8,128]{2,1,0:T(8,128)} %bitcast.21), channel_id=1, replica_groups=mesh['x'=8,'zl'=4,'core'=2,'tp'=8,'pp'=2] {'zl','core'}, dimensions={0} | all-to-all | bytes 65536 | tf_op jit(solution)/shard_map/all_to_all | solution.py:101
  28.4 0.6 tile.4
  29.0 6.1 %all-to-all-start.1 = ((f32[8,8,128]{2,1,0:T(8,128)}), f32[8,8,128]{2,1,0:T(8,128)S(1)}, u32[]{:S(2)}, u32[]{:S(2)}) async-start(f32[8,8,128]{2,1,0:T(8,128)} %tile.4), calls=%async_computation.1 | async-start | bytes 65536 | tf_op jit(solution)/shard_map/all_to_all | solution.py:101
  35.1 0.0 copy-done
  35.2 2.3 %collective-permute-start = (bf16[128,1024]{1,0:T(8,128)(2,1)S(1)}, bf16[128,1024]{1,0:T(8,128)(2,1)S(1)}, u32[]{:S(2)}, u32[]{:S(2)}) collective-permute-start(bf16[128,1024]{1,0:T(8,128)(2,1)S(1)} %copy-done), channel_id=1, source_target_pairs={{16,0},{32,16},{48,32},{64,48},{80,64},{96,80},{112,96},{128,112},... | collective-permute-start | bytes 786440 | tf_op jit(solution)/shard_map/ppermute | solution.py:125
  37.5 5.7 %all-to-all-done.1 = f32[8,8,128]{2,1,0:T(8,128)S(1)} async-done(((f32[8,8,128]{2,1,0:T(8,128)}), f32[8,8,128]{2,1,0:T(8,128)S(1)}, u32[]{:S(2)}, u32[]{:S(2)}) %all-to-all-start.1) | async-done | bytes 32800 | tf_op jit(solution)/shard_map/all_to_all | solution.py:101
  43.2 15.1 %all_to_all.27 = f32[8,1,128]{2,1,0:T(1,128)S(1)} all-to-all(f32[8,1,128]{2,1,0:T(1,128)S(1)} %tile.5), channel_id=1, replica_groups=mesh['x'=8,'zl'=4,'core'=2,'tp'=8,'pp'=2] {'tp'}, dimensions={0} | all-to-all | bytes 8192 | tf_op jit(solution)/shard_map/all_to_all | solution.py:101
  58.3 0.7 broadcast_in_dim.23
  59.0 12.6 %all-to-all-start.3 = ((f32[16,9,128]{2,1,0:T(8,128)}), f32[16,9,128]{2,1,0:T(8,128)S(1)}, u32[]{:S(2)}, u32[]{:S(2)}) async-start(f32[16,9,128]{2,1,0:T(8,128)} %broadcast_in_dim.23), calls=%async_computation.3 | async-start | bytes 262144 | tf_op jit(solution)/shard_map/all_to_all | solution.py:161
  71.6 0.0 collective-permute-done.hw_ref
  71.6 0.0 copy-start.2
  71.6 0.7 copy-done.2
  72.3 5.4 %shard_map.85 = (bf16[128,1024]{1,0:T(8,128)(2,1)}, bf16[128,1024]{1,0:T(8,128)(2,1)}, bf16[128,1024]{1,0:T(8,128)(2,1)}) custom-call(f32[64,128]{1,0:T(8,128)} %bitcast.24, bf16[128,1024]{1,0:T(8,128)(2,1)} %get-tuple-element.9.w_ref, bf16[128,1024]{1,0:T(8,128)(2,1)} %copy-done.2, bf16[128,1024]{1,0:T(8,128)(2,1)} %get-tuple-element.10.p_ref, ...), custom_call_target="tpu_custom_call" | custom-call | flops 1073741824 | bytes 2621440 | tf_op jit(solution)/shard_map/pallas_call | solution.py:136
  77.6 1.3 %collective-permute-start.2 = (bf16[128,1024]{1,0:T(8,128)(2,1)}, bf16[128,1024]{1,0:T(8,128)(2,1)S(1)}, u32[]{:S(2)}, u32[]{:S(2)}) collective-permute-start(bf16[128,1024]{1,0:T(8,128)(2,1)} %get-tuple-element.13), channel_id=1, source_target_pairs={{1,0},{3,2},{5,4},{7,6},{9,8},{11,10},{13,12},{15,14},{17,16},{19,... | collective-permute-start | bytes 786440 | tf_op jit(solution)/shard_map/ppermute | solution.py:144
  78.9 0.0 all-to-all-done.3
  78.9 0.6 slice_reduce_fusion
  80.3 0.6 fusion
  80.9 16.7 %collective-permute-done.2 = bf16[128,1024]{1,0:T(8,128)(2,1)S(1)} collective-permute-done((bf16[128,1024]{1,0:T(8,128)(2,1)}, bf16[128,1024]{1,0:T(8,128)(2,1)S(1)}, u32[]{:S(2)}, u32[]{:S(2)}) %collective-permute-start.2) | collective-permute-done | bytes 262176 | tf_op jit(solution)/shard_map/ppermute | solution.py:144
  97.6 0.7 copy.11
  (8 shorter events, 0.1 us)
Async XLA Ops:
  2.8 7.9 %collective-permute-start.1 = (bf16[128,1024]{1,0:T(8,128)(2,1)}, bf16[128,1024]{1,0:T(8,128)(2,1)S(1)}, u32[]{:S(2)}, u32[]{:S(2)}) collective-permute-start(bf16[128,1024]{1,0:T(8,128)(2,1)} %get-tuple-element.10.p_ref), channel_id=1, source_target_pairs={{0,16},{16,32},{32,48},{48,64},{64,80},{80,96},{96,112},{112,128},... | collective-permute-start | bytes 786440 | tf_op jit(solution)/shard_map/ppermute | solution.py:124
  10.7 0.7 copy-start.1
  11.4 23.8 %copy-start = (bf16[128,1024]{1,0:T(8,128)(2,1)S(1)}, bf16[128,1024]{1,0:T(8,128)(2,1)}, u32[]{:S(2)}) copy-start(bf16[128,1024]{1,0:T(8,128)(2,1)} %get-tuple-element.9.w_ref) | copy-start | bytes 786436
  29.0 14.2 %all-to-all-start.1 = ((f32[8,8,128]{2,1,0:T(8,128)}), f32[8,8,128]{2,1,0:T(8,128)S(1)}, u32[]{:S(2)}, u32[]{:S(2)}) async-start(f32[8,8,128]{2,1,0:T(8,128)} %tile.4), calls=%async_computation.1 | async-start | bytes 65536 | tf_op jit(solution)/shard_map/all_to_all | solution.py:101
  35.2 36.4 %collective-permute-start = (bf16[128,1024]{1,0:T(8,128)(2,1)S(1)}, bf16[128,1024]{1,0:T(8,128)(2,1)S(1)}, u32[]{:S(2)}, u32[]{:S(2)}) collective-permute-start(bf16[128,1024]{1,0:T(8,128)(2,1)S(1)} %copy-done), channel_id=1, source_target_pairs={{16,0},{32,16},{48,32},{64,48},{80,64},{96,80},{112,96},{128,112},... | collective-permute-start | bytes 786440 | tf_op jit(solution)/shard_map/ppermute | solution.py:125
  59.0 20.0 %all-to-all-start.3 = ((f32[16,9,128]{2,1,0:T(8,128)}), f32[16,9,128]{2,1,0:T(8,128)S(1)}, u32[]{:S(2)}, u32[]{:S(2)}) async-start(f32[16,9,128]{2,1,0:T(8,128)} %broadcast_in_dim.23), calls=%async_computation.3 | async-start | bytes 262144 | tf_op jit(solution)/shard_map/all_to_all | solution.py:161
  71.6 0.7 copy-start.2
  77.6 19.9 %collective-permute-start.2 = (bf16[128,1024]{1,0:T(8,128)(2,1)}, bf16[128,1024]{1,0:T(8,128)(2,1)S(1)}, u32[]{:S(2)}, u32[]{:S(2)}) collective-permute-start(bf16[128,1024]{1,0:T(8,128)(2,1)} %get-tuple-element.13), channel_id=1, source_target_pairs={{1,0},{3,2},{5,4},{7,6},{9,8},{11,10},{13,12},{15,14},{17,16},{19,... | collective-permute-start | bytes 786440 | tf_op jit(solution)/shard_map/ppermute | solution.py:144

commit v2 on v1

--- a/solution.py
+++ b/solution.py
@@ -1,3 +1,4 @@
+import functools
 import math
 
 import jax
@@ -15,6 +16,7 @@
 PER_BLOCK = LANES // GROUP
 
 CTX = ("x", "zl", "core")
+VMEM_LIMIT = 16 * 1024 * 1024
 BF16 = jnp.bfloat16
 F32 = jnp.float32
 
@@ -55,7 +57,8 @@
             part = pairs[g * LANES : (g + 1) * LANES]
             part = jnp.where(own, part[:, :LANES], part[:, LANES:])
             part = pltpu.roll(part, 1, 1, stride=1, stride_axis=0)
-            raw_ref[pl.ds(block * PER_BLOCK + g, 1), :] = jnp.sum(part, axis=0, keepdims=True)
+            spot = pl.ds(g * (raw_ref.shape[0] // PER_BLOCK) + block, 1)
+            raw_ref[spot, :] = jnp.sum(part, axis=0, keepdims=True)
 
 
 def mix_kernel(
@@ -97,6 +100,50 @@
         gq_ref[:, lanes] = dot(flip, (cot * ahead).astype(BF16)).astype(BF16)
 
 
+def settle_kernel(*refs):
+    half = len(refs) // 2
+    for in_ref, out_ref in zip(refs[:half], refs[half:]):
+        out_ref[...] = in_ref[...]
+
+
+def settle(*arrays):
+    size = sum(a.size * a.dtype.itemsize for a in arrays)
+    return pl.pallas_call(
+        settle_kernel,
+        out_shape=tuple(jax.ShapeDtypeStruct(a.shape, a.dtype) for a in arrays),
+        compiler_params=pltpu.CompilerParams(vmem_limit_bytes=VMEM_LIMIT),
+        cost_estimate=pl.CostEstimate(flops=0, bytes_accessed=2 * size, transcendentals=0),
+    )(*[near_in(a) for a in arrays])
+
+
+def pack_kernel(part_ref, squares_ref, packed_ref):
+    squares = jnp.sum(squares_ref[...], axis=0, keepdims=True)
+    share, taps = part_ref.shape
+    for member in range(packed_ref.shape[0]):
+        for row in range(share):
+            packed_ref[member, :, pl.ds(row * taps, taps)] = part_ref[pl.ds(row, 1), :]
+        packed_ref[member, :, pl.ds(share * taps, taps)] = squares
+
+
+def clip_kernel(clip_level, packed_ref, grad_ref):
+    members, _, width = packed_ref.shape
+    squares = packed_ref[0, :, pl.ds(width - TAPS, TAPS)]
+    for member in range(1, members):
+        squares += packed_ref[member, :, pl.ds(width - TAPS, TAPS)]
+    norm = jnp.sqrt(jnp.sum(squares, axis=1, keepdims=True))
+    factor = jnp.minimum(1.0, clip_level / (norm + 1e-06))
+    near = members // lax.axis_size("pp")
+    first = lax.axis_index("pp") * near
+    for row in range(width // TAPS - 1):
+        for member in range(near):
+            own = packed_ref[first + member, :, pl.ds(row * TAPS, TAPS)]
+            grad_ref[pl.ds(row * near + member, 1), :] = own * factor
+
+
+def near_in(x):
+    return pltpu.with_memory_space_constraint(x, pltpu.VMEM)
+
+
 def exchange(rows, axes):
     return lax.all_to_all(rows, axes, 0, 0, tiled=True)
 
@@ -109,12 +156,12 @@
 def block(q, k, v, c, filters):
     length, channels = q.shape
     groups_here = filters.shape[0]
-    whole = jax.ShapeDtypeStruct((length, channels), BF16)
+    inner = pltpu.VMEM((length, channels), BF16)
     size = length * channels * 2
 
     prod, weighted = pl.pallas_call(
         products_kernel,
-        out_shape=(whole, whole),
+        out_shape=(inner, inner),
         cost_estimate=pl.CostEstimate(
             flops=2 * LANES * length * channels, bytes_accessed=6 * size, transcendentals=0
         ),
@@ -126,22 +173,26 @@
 
     raw = pl.pallas_call(
         filter_grad_kernel,
-        out_shape=jax.ShapeDtypeStruct((groups_here, TAPS), F32),
+        out_shape=pltpu.VMEM((groups_here, TAPS), F32),
         scratch_shapes=[pltpu.VMEM((PER_BLOCK * LANES, LANES), BF16)],
+        compiler_params=pltpu.CompilerParams(vmem_limit_bytes=VMEM_LIMIT),
         cost_estimate=pl.CostEstimate(
             flops=4 * groups_here * LANES**3, bytes_accessed=3 * size, transcendentals=0
         ),
-    )(weighted, prod, behind)
+    )(near_in(weighted), near_in(prod), near_in(behind))
 
     grad_q, grad_k, dvalues = pl.pallas_call(
         mix_kernel,
-        out_shape=(whole, whole, whole),
+        out_shape=(inner, inner, inner),
         scratch_shapes=[pltpu.VMEM((PER_BLOCK * LANES, 2 * LANES), BF16)],
+        compiler_params=pltpu.CompilerParams(vmem_limit_bytes=VMEM_LIMIT),
         cost_estimate=pl.CostEstimate(
             flops=8 * groups_here * LANES**3, bytes_accessed=10 * size, transcendentals=0
         ),
-    )(filters, weighted, ahead, prod, behind, c, k, v)
+    )(filters, near_in(weighted), near_in(ahead), near_in(prod), near_in(behind), near_in(c), near_in(k), near_in(v))
     handed = lax.ppermute(dvalues, "pp", [(1, 0)])
+    (handed,) = settle(handed)
+    grad_q, grad_k = settle(grad_q, grad_k)
 
     near = lax.axis_size(("zl", "core"))
     share = groups_here // near
@@ -151,19 +202,23 @@
     part = jnp.tile(part, (wide, 1))
     part = exchange(part, "x")
     part = jnp.sum(part.reshape(wide, share, TAPS), axis=0)
-    square = jnp.sum(part * part, axis=0, keepdims=True)
-    square = jnp.tile(square, (lax.axis_size("tp"), 1))
-    square = exchange(square, "tp")
-    square = jnp.sum(square, axis=0, keepdims=True)
+    squares = jnp.sum(part * part, axis=0, keepdims=True)
+    squares = jnp.tile(squares, (lax.axis_size("tp"), 1))
+    squares = exchange(squares, "tp")
     line = ("pp", "zl", "core")
-    packed = jnp.concatenate([part, square], axis=0)
-    packed = jnp.broadcast_to(packed[None], (lax.axis_size(line), share + 1, TAPS))
-    packed = lax.all_to_all(packed, line, 0, 0)
-    norm_sq = jnp.sum(packed[:, share])
+    members = lax.axis_size(line)
+    packed = pl.pallas_call(
+        pack_kernel,
+        out_shape=jax.ShapeDtypeStruct((members, 1, (share + 1) * TAPS), F32),
+        compiler_params=pltpu.CompilerParams(vmem_limit_bytes=VMEM_LIMIT),
+    )(near_in(part), near_in(squares))
+    packed = lax.all_to_all(packed, line, 0, 0, tiled=True)
     clip_level = 0.25 * math.sqrt(lax.axis_size("pp") * GROUPS * TAPS)
-    factor = jnp.minimum(1.0, clip_level / (jnp.sqrt(norm_sq) + 1e-06))
-    summed = lax.dynamic_slice_in_dim(packed, lax.axis_index("pp") * near, near, 0)
-    grad_f = summed[:, :share].reshape(groups_here, TAPS) * factor
+    grad_f = pl.pallas_call(
+        functools.partial(clip_kernel, clip_level),
+        out_shape=jax.ShapeDtypeStruct((groups_here, TAPS), F32),
+        compiler_params=pltpu.CompilerParams(vmem_limit_bytes=VMEM_LIMIT),
+    )(near_in(packed))
     return grad_q, grad_k, handed, grad_f
 
 

time: 98.8 us -> 80.8 us (0.82)
  the two profiles are of different devices: /device:TPU:128 before, /device:TPU:1 now
where the time goes in v2:
time: 80.8 us; the launch traced here: 80.3 us
  starting transfers between devices  39.6 us (49%)
  blocking collectives  20.6 us (25%)
  waiting for transfers between devices  9.46 us (12%)
  Pallas kernels  9.12 us (11%)
    all_to_all x2, blocking collectives, exchange(): return lax.all_to_all(rows, axes, 0, 0, tiled=True)  20.6 us
    all_to_all x1, starting transfers between devices, block(): packed = lax.all_to_all(packed, line, 0, 0, tiled=True)  14.6 us
    ppermute x1, starting transfers between devices, block(): ahead = lax.ppermute(weighted, CTX, [(i + 1, i) for i in range(count - 1)])  11.2 us
    all_to_all x1, waiting for transfers between devices, block(): packed = lax.all_to_all(packed, line, 0, 0, tiled=True)  7.12 us
    all_to_all x1, starting transfers between devices, exchange(): return lax.all_to_all(rows, axes, 0, 0, tiled=True)  6.31 us
    ppermute x1, starting transfers between devices, block(): behind = lax.ppermute(prod, CTX, [(i, i + 1) for i in range(count - 1)])  6.29 us
    pallas_call x1, Pallas kernels, block(): pl.pallas_call(mix_kernel, out_shape=(inner, inner, inner), scratch_shape...  3.19 us
    all_to_all x1, waiting for transfers between devices, exchange(): return lax.all_to_all(rows, axes, 0, 0, tiled=True)  2.34 us
  transfers between devices with their start and end apart: 5, of which 2 were waited for; matrix products, arithmetic and copies ran while one was open for 1% of the time, Pallas kernels for 9%

profile of v2, /device:TPU:1, one launch (start us, length us, event | category | flops | bytes accessed | tf_op | source)
XLA Modules:
  0.0 80.3 jit_solution(5153627780864003444)
XLA Ops:
  0.6 1.4 %shard_map.84 = (bf16[128,1024]{1,0:T(8,128)(2,1)S(1)}, bf16[128,1024]{1,0:T(8,128)(2,1)S(1)}) custom-call(bf16[128,1024]{1,0:T(8,128)(2,1)} %bitcast.11, bf16[128,1024]{1,0:T(8,128)(2,1)} %bitcast.13, bf16[128,1024]{1,0:T(8,128)(2,1)} %bitcast.15, bf16[128,1024]{1,0:T(8,128)(2,1)} %bitcast.21), custom_call_target="tpu_custom_call" | custom-call | flops 33554432 | bytes 1572864 | tf_op jit(solution)/shard_map/pallas_call | solution.py:162
  2.1 6.3 %collective-permute-start.1 = (bf16[128,1024]{1,0:T(8,128)(2,1)S(1)}, bf16[128,1024]{1,0:T(8,128)(2,1)S(1)}, u32[]{:S(2)}, u32[]{:S(2)}) collective-permute-start(bf16[128,1024]{1,0:T(8,128)(2,1)S(1)} %get-tuple-element.12.p_ref), channel_id=1, source_target_pairs={{0,16},{16,32},{32,48},{48,64},{64,80},{80,96},{96,112},{112,128},... | collective-permute-start | bytes 786440 | tf_op jit(solution)/shard_map/ppermute | solution.py:171
  8.4 0.0 copy-start
  8.4 0.0 copy-start.1
  8.4 0.0 copy-start.2
  8.4 11.2 %collective-permute-start = (bf16[128,1024]{1,0:T(8,128)(2,1)S(1)}, bf16[128,1024]{1,0:T(8,128)(2,1)S(1)}, u32[]{:S(2)}, u32[]{:S(2)}) collective-permute-start(bf16[128,1024]{1,0:T(8,128)(2,1)S(1)} %get-tuple-element.11.w_ref), channel_id=1, source_target_pairs={{16,0},{32,16},{48,32},{64,48},{80,64},{96,80},{112,96},{128,112},... | collective-permute-start | bytes 786440 | tf_op jit(solution)/shard_map/ppermute | solution.py:172
  19.6 0.0 collective-permute-done.1.hp_ref
  19.6 1.5 %shard_map.88 = f32[64,128]{1,0:T(8,128)S(1)} custom-call(bf16[128,1024]{1,0:T(8,128)(2,1)S(1)} %get-tuple-element.11.w_ref, bf16[128,1024]{1,0:T(8,128)(2,1)S(1)} %get-tuple-element.12.p_ref, bf16[128,1024]{1,0:T(8,128)(2,1)S(1)} %collective-permute-done.1.hp_ref), custom_call_target="tpu_custom_call" | custom-call | flops 536870912 | bytes 786432 | tf_op jit(solution)/shard_map/pallas_call | solution.py:174
  21.1 6.7 %all_to_all.28 = f32[8,8,128]{2,1,0:T(8,128)S(1)} all-to-all(f32[8,8,128]{2,1,0:T(8,128)S(1)} %bitcast.17), channel_id=1, replica_groups=mesh['x'=8,'zl'=4,'core'=2,'tp'=8,'pp'=2] {'zl','core'}, dimensions={0} | all-to-all | bytes 65536 | tf_op jit(solution)/shard_map/all_to_all | solution.py:148
  27.9 0.6 tile.4
  28.5 6.3 %all-to-all-start.1 = ((f32[8,8,128]{2,1,0:T(8,128)}), f32[8,8,128]{2,1,0:T(8,128)S(1)}, u32[]{:S(2)}, u32[]{:S(2)}) async-start(f32[8,8,128]{2,1,0:T(8,128)} %tile.4), calls=%async_computation.1 | async-start | bytes 65536 | tf_op jit(solution)/shard_map/all_to_all | solution.py:148
  34.8 0.0 collective-permute-done.hw_ref
  34.8 0.0 copy-done
  34.8 3.2 %shard_map.85 = (bf16[128,1024]{1,0:T(8,128)(2,1)S(1)}, bf16[128,1024]{1,0:T(8,128)(2,1)S(1)}, bf16[128,1024]{1,0:T(8,128)(2,1)S(1)}) custom-call(f32[64,128]{1,0:T(8,128)S(1)} %bitcast.19, bf16[128,1024]{1,0:T(8,128)(2,1)S(1)} %get-tuple-element.11.w_ref, bf16[128,1024]{1,0:T(8,128)(2,1)S(1)} %collective-permute-done.hw_ref, ...), custom_call_target="tpu_custom_call" | custom-call | flops 1073741824 | bytes 2621440 | tf_op jit(solution)/shard_map/pallas_call | solution.py:184
  38.0 1.3 %collective-permute-start.2 = (bf16[128,1024]{1,0:T(8,128)(2,1)S(1)}, bf16[128,1024]{1,0:T(8,128)(2,1)S(1)}, u32[]{:S(2)}, u32[]{:S(2)}) collective-permute-start(bf16[128,1024]{1,0:T(8,128)(2,1)S(1)} %get-tuple-element.17), channel_id=1, source_target_pairs={{1,0},{3,2},{5,4},{7,6},{9,8},{11,10},{13,12},{15,14},{17,16},{19,... | collective-permute-start | bytes 786440 | tf_op jit(solution)/shard_map/ppermute | solution.py:193
  39.3 2.3 %all-to-all-done.1 = f32[8,8,128]{2,1,0:T(8,128)S(1)} async-done(((f32[8,8,128]{2,1,0:T(8,128)}), f32[8,8,128]{2,1,0:T(8,128)S(1)}, u32[]{:S(2)}, u32[]{:S(2)}) %all-to-all-start.1) | async-done | bytes 32800 | tf_op jit(solution)/shard_map/all_to_all | solution.py:148
  41.7 13.9 %all_to_all.29 = f32[8,1,128]{2,1,0:T(1,128)S(1)} all-to-all(f32[8,1,128]{2,1,0:T(1,128)S(1)} %tile.5), channel_id=1, replica_groups=mesh['x'=8,'zl'=4,'core'=2,'tp'=8,'pp'=2] {'tp'}, dimensions={0} | all-to-all | bytes 8192 | tf_op jit(solution)/shard_map/all_to_all | solution.py:148
  55.6 0.7 shard_map.89
  56.3 14.6 %all-to-all-start.3 = ((f32[16,1,1152]{2,1,0:T(1,128)}), f32[16,1,1152]{2,1,0:T(1,128)S(1)}, u32[]{:S(2)}, u32[]{:S(2)}) async-start(f32[16,1,1152]{2,1,0:T(1,128)} %shard_map.89), calls=%async_computation.3 | async-start | bytes 147456 | tf_op jit(solution)/shard_map/all_to_all | solution.py:215
  70.9 0.8 %shard_map.86 = (bf16[128,1024]{1,0:T(8,128)(2,1)}, bf16[128,1024]{1,0:T(8,128)(2,1)}) custom-call(bf16[128,1024]{1,0:T(8,128)(2,1)S(1)} %get-tuple-element.13.refs_0_, bf16[128,1024]{1,0:T(8,128)(2,1)S(1)} %get-tuple-element.14.refs_1_), custom_call_target="tpu_custom_call" | custom-call | bytes 1048576 | tf_op jit(solution)/shard_map/pallas_call | solution.py:111
  71.7 7.1 %all-to-all-done.3.packed_ref = f32[16,1,1152]{2,1,0:T(1,128)S(1)} async-done(((f32[16,1,1152]{2,1,0:T(1,128)}), f32[16,1,1152]{2,1,0:T(1,128)S(1)}, u32[]{:S(2)}, u32[]{:S(2)}) %all-to-all-start.3) | async-done | bytes 73760 | tf_op jit(solution)/shard_map/all_to_all | solution.py:215
  78.8 0.7 shard_map.90
  79.6 0.0 collective-permute-done.2.refs_0_
  79.6 0.7 shard_map.87
  (8 shorter events, 0.1 us)
Async XLA Ops:
  2.1 17.5 %collective-permute-start.1 = (bf16[128,1024]{1,0:T(8,128)(2,1)S(1)}, bf16[128,1024]{1,0:T(8,128)(2,1)S(1)}, u32[]{:S(2)}, u32[]{:S(2)}) collective-permute-start(bf16[128,1024]{1,0:T(8,128)(2,1)S(1)} %get-tuple-element.12.p_ref), channel_id=1, source_target_pairs={{0,16},{16,32},{32,48},{48,64},{64,80},{80,96},{96,112},{112,128},... | collective-permute-start | bytes 786440 | tf_op jit(solution)/shard_map/ppermute | solution.py:171
  8.4 26.4 %copy-start = (bf16[1,128,1024]{2,1,0:T(8,128)(2,1)S(1)}, bf16[1,128,1024]{2,1,0:T(8,128)(2,1)}, u32[]{:S(2)}) copy-start(bf16[1,128,1024]{2,1,0:T(8,128)(2,1)} %param.6) | copy-start | bytes 786436
  8.4 26.4 %copy-start.1 = (bf16[1,128,1024]{2,1,0:T(8,128)(2,1)S(1)}, bf16[1,128,1024]{2,1,0:T(8,128)(2,1)}, u32[]{:S(2)}) copy-start(bf16[1,128,1024]{2,1,0:T(8,128)(2,1)} %param.7) | copy-start | bytes 786436
  8.4 26.4 %copy-start.2 = (bf16[1,128,1024]{2,1,0:T(8,128)(2,1)S(1)}, bf16[1,128,1024]{2,1,0:T(8,128)(2,1)}, u32[]{:S(2)}) copy-start(bf16[1,128,1024]{2,1,0:T(8,128)(2,1)} %param.8) | copy-start | bytes 786436
  8.4 26.4 %collective-permute-start = (bf16[128,1024]{1,0:T(8,128)(2,1)S(1)}, bf16[128,1024]{1,0:T(8,128)(2,1)S(1)}, u32[]{:S(2)}, u32[]{:S(2)}) collective-permute-start(bf16[128,1024]{1,0:T(8,128)(2,1)S(1)} %get-tuple-element.11.w_ref), channel_id=1, source_target_pairs={{16,0},{32,16},{48,32},{64,48},{80,64},{96,80},{112,96},{128,112},... | collective-permute-start | bytes 786440 | tf_op jit(solution)/shard_map/ppermute | solution.py:172
  28.5 6.3 %copy-start.3 = (f32[1,64,128]{2,1,0:T(8,128)S(1)}, f32[1,64,128]{2,1,0:T(8,128)}, u32[]{:S(2)}) copy-start(f32[1,64,128]{2,1,0:T(8,128)} %param.9) | copy-start | bytes 98308
  28.5 13.2 %all-to-all-start.1 = ((f32[8,8,128]{2,1,0:T(8,128)}), f32[8,8,128]{2,1,0:T(8,128)S(1)}, u32[]{:S(2)}, u32[]{:S(2)}) async-start(f32[8,8,128]{2,1,0:T(8,128)} %tile.4), calls=%async_computation.1 | async-start | bytes 65536 | tf_op jit(solution)/shard_map/all_to_all | solution.py:148
  38.0 41.5 %collective-permute-start.2 = (bf16[128,1024]{1,0:T(8,128)(2,1)S(1)}, bf16[128,1024]{1,0:T(8,128)(2,1)S(1)}, u32[]{:S(2)}, u32[]{:S(2)}) collective-permute-start(bf16[128,1024]{1,0:T(8,128)(2,1)S(1)} %get-tuple-element.17), channel_id=1, source_target_pairs={{1,0},{3,2},{5,4},{7,6},{9,8},{11,10},{13,12},{15,14},{17,16},{19,... | collective-permute-start | bytes 786440 | tf_op jit(solution)/shard_map/ppermute | solution.py:193
  56.3 22.5 %all-to-all-start.3 = ((f32[16,1,1152]{2,1,0:T(1,128)}), f32[16,1,1152]{2,1,0:T(1,128)S(1)}, u32[]{:S(2)}, u32[]{:S(2)}) async-start(f32[16,1,1152]{2,1,0:T(1,128)} %shard_map.89), calls=%async_computation.3 | async-start | bytes 147456 | tf_op jit(solution)/shard_map/all_to_all | solution.py:215

commit v3 on v2

--- a/solution.py
+++ b/solution.py
@@ -133,7 +133,7 @@
     norm = jnp.sqrt(jnp.sum(squares, axis=1, keepdims=True))
     factor = jnp.minimum(1.0, clip_level / (norm + 1e-06))
     near = members // lax.axis_size("pp")
-    first = lax.axis_index("pp") * near
+    first = members - near - lax.axis_index("pp") * near
     for row in range(width // TAPS - 1):
         for member in range(near):
             own = packed_ref[first + member, :, pl.ds(row * TAPS, TAPS)]
@@ -144,8 +144,12 @@
     return pltpu.with_memory_space_constraint(x, pltpu.VMEM)
 
 
-def exchange(rows, axes):
-    return lax.all_to_all(rows, axes, 0, 0, tiled=True)
+def exchange(rows, axes, order):
+    return lax.all_to_all(rows, axes, 0, 0, tiled=True, axis_index_groups=[order])
+
+
+def from_middle(count):
+    return [(count // 2 + i) % count for i in range(count)]
 
 
 def per_device(queries, key_feats, value_feats, cotangent, filters):
@@ -196,15 +200,18 @@
 
     near = lax.axis_size(("zl", "core"))
     share = groups_here // near
-    part = exchange(raw, ("zl", "core"))
+    cores = lax.axis_size("core")
+    by_near = [zl * cores + core for zl in (1, 2, 0, 3) for core in range(cores)]
+    part = exchange(raw, ("zl", "core"), by_near)
     part = jnp.sum(part.reshape(near, share, TAPS), axis=0)
     wide = lax.axis_size("x")
     part = jnp.tile(part, (wide, 1))
-    part = exchange(part, "x")
+    part = exchange(part, "x", from_middle(wide))
     part = jnp.sum(part.reshape(wide, share, TAPS), axis=0)
     squares = jnp.sum(part * part, axis=0, keepdims=True)
-    squares = jnp.tile(squares, (lax.axis_size("tp"), 1))
-    squares = exchange(squares, "tp")
+    deep = lax.axis_size("tp")
+    squares = jnp.tile(squares, (deep, 1))
+    squares = exchange(squares, "tp", from_middle(deep))
     line = ("pp", "zl", "core")
     members = lax.axis_size(line)
     packed = pl.pallas_call(
@@ -212,7 +219,8 @@
         out_shape=jax.ShapeDtypeStruct((members, 1, (share + 1) * TAPS), F32),
         compiler_params=pltpu.CompilerParams(vmem_limit_bytes=VMEM_LIMIT),
     )(near_in(part), near_in(squares))
-    packed = lax.all_to_all(packed, line, 0, 0, tiled=True)
+    halves = reversed(range(lax.axis_size("pp")))
+    packed = exchange(packed, line, [pp * near + i for pp in halves for i in by_near])
     clip_level = 0.25 * math.sqrt(lax.axis_size("pp") * GROUPS * TAPS)
     grad_f = pl.pallas_call(
         functools.partial(clip_kernel, clip_level),

time: 80.8 us -> 71.1 us (0.88)
  waiting for transfers between devices: 9.46 us -> 3.12 us
  blocking collectives: 20.6 us -> 16.5 us
    all_to_all x2, waiting for transfers between devices: 9.46 us -> 3.11 us  [exchange(): lax.all_to_all(rows, axes, 0, 0, tiled=True, axis_index_groups=[order])]
    all_to_all x2, blocking collectives: 20.6 us -> 16.5 us  [exchange(): lax.all_to_all(rows, axes, 0, 0, tiled=True, axis_index_groups=[order])]
    all_to_all x2, starting transfers between devices: 20.9 us -> 21.7 us  [exchange(): lax.all_to_all(rows, axes, 0, 0, tiled=True, axis_index_groups=[order])]
  transfers between devices with their start and end apart: 5 -> 5, of which waited for: 2 -> 1; matrix products, arithmetic and copies ran while one was open for 1% -> 1% of each run, Pallas kernels for 9% -> 10%
where the time goes in v3:
time: 71.1 us; the launch traced here: 70.6 us
  starting transfers between devices  40.4 us (57%)
  blocking collectives  16.5 us (23%)
  Pallas kernels  9.12 us (13%)
  waiting for transfers between devices  3.12 us (4%)
  between operations  0.75 us (1%)
    all_to_all x2, starting transfers between devices, exchange(): lax.all_to_all(rows, axes, 0, 0, tiled=True, axis_index_groups=[order])  21.7 us
    all_to_all x2, blocking collectives, exchange(): lax.all_to_all(rows, axes, 0, 0, tiled=True, axis_index_groups=[order])  16.5 us
    ppermute x1, starting transfers between devices, block(): ahead = lax.ppermute(weighted, CTX, [(i + 1, i) for i in range(count - 1)])  11.2 us
    ppermute x1, starting transfers between devices, block(): behind = lax.ppermute(prod, CTX, [(i, i + 1) for i in range(count - 1)])  6.29 us
    pallas_call x1, Pallas kernels, block(): pl.pallas_call(mix_kernel, out_shape=(inner, inner, inner), scratch_shape...  3.19 us
    all_to_all x2, waiting for transfers between devices, exchange(): lax.all_to_all(rows, axes, 0, 0, tiled=True, axis_index_groups=[order])  3.11 us
    pallas_call x2, Pallas kernels, settle(): pl.pallas_call(settle_kernel, out_shape=tuple((jax.ShapeDtypeStruct(a.sha...  1.54 us
    pallas_call x1, Pallas kernels, block(): pl.pallas_call(filter_grad_kernel, out_shape=pltpu.VMEM((groups_here, TAP...  1.54 us
  transfers between devices with their start and end apart: 5, of which 1 were waited for; matrix products, arithmetic and copies ran while one was open for 1% of the time, Pallas kernels for 10%

profile of v3, /device:TPU:1, one launch (start us, length us, event | category | flops | bytes accessed | tf_op | source)
XLA Modules:
  0.0 70.6 jit_solution(14744349681732316688)
XLA Ops:
  0.6 1.4 %shard_map.84 = (bf16[128,1024]{1,0:T(8,128)(2,1)S(1)}, bf16[128,1024]{1,0:T(8,128)(2,1)S(1)}) custom-call(bf16[128,1024]{1,0:T(8,128)(2,1)} %bitcast.11, bf16[128,1024]{1,0:T(8,128)(2,1)} %bitcast.13, bf16[128,1024]{1,0:T(8,128)(2,1)} %bitcast.15, bf16[128,1024]{1,0:T(8,128)(2,1)} %bitcast.21), custom_call_target="tpu_custom_call" | custom-call | flops 33554432 | bytes 1572864 | tf_op jit(solution)/shard_map/pallas_call | solution.py:166
  2.1 6.3 %collective-permute-start.1 = (bf16[128,1024]{1,0:T(8,128)(2,1)S(1)}, bf16[128,1024]{1,0:T(8,128)(2,1)S(1)}, u32[]{:S(2)}, u32[]{:S(2)}) collective-permute-start(bf16[128,1024]{1,0:T(8,128)(2,1)S(1)} %get-tuple-element.12.p_ref), channel_id=1, source_target_pairs={{0,16},{16,32},{32,48},{48,64},{64,80},{80,96},{96,112},{112,128},... | collective-permute-start | bytes 786440 | tf_op jit(solution)/shard_map/ppermute | solution.py:175
  8.4 0.0 copy-start
  8.4 0.0 copy-start.1
  8.4 0.0 copy-start.2
  8.4 11.2 %collective-permute-start = (bf16[128,1024]{1,0:T(8,128)(2,1)S(1)}, bf16[128,1024]{1,0:T(8,128)(2,1)S(1)}, u32[]{:S(2)}, u32[]{:S(2)}) collective-permute-start(bf16[128,1024]{1,0:T(8,128)(2,1)S(1)} %get-tuple-element.11.w_ref), channel_id=1, source_target_pairs={{16,0},{32,16},{48,32},{64,48},{80,64},{96,80},{112,96},{128,112},... | collective-permute-start | bytes 786440 | tf_op jit(solution)/shard_map/ppermute | solution.py:176
  19.6 0.0 collective-permute-done.1.hp_ref
  19.6 1.5 %shard_map.88 = f32[64,128]{1,0:T(8,128)S(1)} custom-call(bf16[128,1024]{1,0:T(8,128)(2,1)S(1)} %get-tuple-element.11.w_ref, bf16[128,1024]{1,0:T(8,128)(2,1)S(1)} %get-tuple-element.12.p_ref, bf16[128,1024]{1,0:T(8,128)(2,1)S(1)} %collective-permute-done.1.hp_ref), custom_call_target="tpu_custom_call" | custom-call | flops 536870912 | bytes 786432 | tf_op jit(solution)/shard_map/pallas_call | solution.py:178
  21.1 6.7 %all_to_all.28 = f32[8,8,128]{2,1,0:T(8,128)S(1)} all-to-all(f32[8,8,128]{2,1,0:T(8,128)S(1)} %bitcast.17), channel_id=1, replica_groups={{32,48,64,80,0,16,96,112},{33,49,65,81,1,17,97,113},{34,50,66,82,2,18,9..., dimensions={0} | all-to-all | bytes 65536 | tf_op jit(solution)/shard_map/all_to_all | solution.py:148
  27.8 0.6 tile.4
  28.4 7.4 %all-to-all-start.1 = ((f32[8,8,128]{2,1,0:T(8,128)}), f32[8,8,128]{2,1,0:T(8,128)S(1)}, u32[]{:S(2)}, u32[]{:S(2)}) async-start(f32[8,8,128]{2,1,0:T(8,128)} %tile.4), calls=%async_computation.1 | async-start | bytes 65536 | tf_op jit(solution)/shard_map/all_to_all | solution.py:148
  35.8 0.0 collective-permute-done.hw_ref
  35.9 0.0 copy-done.1
  35.9 3.2 %shard_map.85 = (bf16[128,1024]{1,0:T(8,128)(2,1)S(1)}, bf16[128,1024]{1,0:T(8,128)(2,1)S(1)}, bf16[128,1024]{1,0:T(8,128)(2,1)S(1)}) custom-call(f32[64,128]{1,0:T(8,128)S(1)} %bitcast.19, bf16[128,1024]{1,0:T(8,128)(2,1)S(1)} %get-tuple-element.11.w_ref, bf16[128,1024]{1,0:T(8,128)(2,1)S(1)} %collective-permute-done.hw_ref, ...), custom_call_target="tpu_custom_call" | custom-call | flops 1073741824 | bytes 2621440 | tf_op jit(solution)/shard_map/pallas_call | solution.py:188
  39.1 1.3 %collective-permute-start.2 = (bf16[128,1024]{1,0:T(8,128)(2,1)S(1)}, bf16[128,1024]{1,0:T(8,128)(2,1)S(1)}, u32[]{:S(2)}, u32[]{:S(2)}) collective-permute-start(bf16[128,1024]{1,0:T(8,128)(2,1)S(1)} %get-tuple-element.17), channel_id=1, source_target_pairs={{1,0},{3,2},{5,4},{7,6},{9,8},{11,10},{13,12},{15,14},{17,16},{19,... | collective-permute-start | bytes 786440 | tf_op jit(solution)/shard_map/ppermute | solution.py:197
  40.4 0.0 all-to-all-done.1
  40.4 9.8 %all_to_all.29 = f32[8,1,128]{2,1,0:T(1,128)S(1)} all-to-all(f32[8,1,128]{2,1,0:T(1,128)S(1)} %tile.5), channel_id=1, replica_groups={{8,10,12,14,0,2,4,6},{9,11,13,15,1,3,5,7},{24,26,28,30,16,18,20,22},{25..., dimensions={0} | all-to-all | bytes 8192 | tf_op jit(solution)/shard_map/all_to_all | solution.py:148
  50.3 0.7 shard_map.89
  50.9 14.3 %all-to-all-start.3 = ((f32[16,1,1152]{2,1,0:T(1,128)}), f32[16,1,1152]{2,1,0:T(1,128)S(1)}, u32[]{:S(2)}, u32[]{:S(2)}) async-start(f32[16,1,1152]{2,1,0:T(1,128)} %shard_map.89), calls=%async_computation.3 | async-start | bytes 147456 | tf_op jit(solution)/shard_map/all_to_all | solution.py:148
  65.2 0.8 %shard_map.86 = (bf16[128,1024]{1,0:T(8,128)(2,1)}, bf16[128,1024]{1,0:T(8,128)(2,1)}) custom-call(bf16[128,1024]{1,0:T(8,128)(2,1)S(1)} %get-tuple-element.13.refs_0_, bf16[128,1024]{1,0:T(8,128)(2,1)S(1)} %get-tuple-element.14.refs_1_), custom_call_target="tpu_custom_call" | custom-call | bytes 1048576 | tf_op jit(solution)/shard_map/pallas_call | solution.py:111
  66.0 3.1 %all-to-all-done.3.packed_ref = f32[16,1,1152]{2,1,0:T(1,128)S(1)} async-done(((f32[16,1,1152]{2,1,0:T(1,128)}), f32[16,1,1152]{2,1,0:T(1,128)S(1)}, u32[]{:S(2)}, u32[]{:S(2)}) %all-to-all-start.3) | async-done | bytes 73760 | tf_op jit(solution)/shard_map/all_to_all | solution.py:148
  69.2 0.7 %shard_map.90 = f32[64,128]{1,0:T(8,128)} custom-call(f32[16,1,1152]{2,1,0:T(1,128)S(1)} %all-to-all-done.3.packed_ref), custom_call_target="tpu_custom_call" | custom-call | tf_op jit(solution)/shard_map/pallas_call | solution.py:225
  69.9 0.0 collective-permute-done.2.refs_0_
  69.9 0.7 %shard_map.87 = bf16[128,1024]{1,0:T(8,128)(2,1)} custom-call(bf16[128,1024]{1,0:T(8,128)(2,1)S(1)} %collective-permute-done.2.refs_0_), custom_call_target="tpu_custom_call" | custom-call | bytes 524288 | tf_op jit(solution)/shard_map/pallas_call | solution.py:111
  (8 shorter events, 0.1 us)
Async XLA Ops:
  2.1 17.5 %collective-permute-start.1 = (bf16[128,1024]{1,0:T(8,128)(2,1)S(1)}, bf16[128,1024]{1,0:T(8,128)(2,1)S(1)}, u32[]{:S(2)}, u32[]{:S(2)}) collective-permute-start(bf16[128,1024]{1,0:T(8,128)(2,1)S(1)} %get-tuple-element.12.p_ref), channel_id=1, source_target_pairs={{0,16},{16,32},{32,48},{48,64},{64,80},{80,96},{96,112},{112,128},... | collective-permute-start | bytes 786440 | tf_op jit(solution)/shard_map/ppermute | solution.py:175
  8.4 27.5 %copy-start = (bf16[1,128,1024]{2,1,0:T(8,128)(2,1)S(1)}, bf16[1,128,1024]{2,1,0:T(8,128)(2,1)}, u32[]{:S(2)}) copy-start(bf16[1,128,1024]{2,1,0:T(8,128)(2,1)} %param.6) | copy-start | bytes 786436
  8.4 27.5 %copy-start.1 = (bf16[1,128,1024]{2,1,0:T(8,128)(2,1)S(1)}, bf16[1,128,1024]{2,1,0:T(8,128)(2,1)}, u32[]{:S(2)}) copy-start(bf16[1,128,1024]{2,1,0:T(8,128)(2,1)} %param.7) | copy-start | bytes 786436
  8.4 27.5 %copy-start.2 = (bf16[1,128,1024]{2,1,0:T(8,128)(2,1)S(1)}, bf16[1,128,1024]{2,1,0:T(8,128)(2,1)}, u32[]{:S(2)}) copy-start(bf16[1,128,1024]{2,1,0:T(8,128)(2,1)} %param.8) | copy-start | bytes 786436
  8.4 27.4 %collective-permute-start = (bf16[128,1024]{1,0:T(8,128)(2,1)S(1)}, bf16[128,1024]{1,0:T(8,128)(2,1)S(1)}, u32[]{:S(2)}, u32[]{:S(2)}) collective-permute-start(bf16[128,1024]{1,0:T(8,128)(2,1)S(1)} %get-tuple-element.11.w_ref), channel_id=1, source_target_pairs={{16,0},{32,16},{48,32},{64,48},{80,64},{96,80},{112,96},{128,112},... | collective-permute-start | bytes 786440 | tf_op jit(solution)/shard_map/ppermute | solution.py:176
  28.4 7.4 %copy-start.3 = (f32[1,64,128]{2,1,0:T(8,128)S(1)}, f32[1,64,128]{2,1,0:T(8,128)}, u32[]{:S(2)}) copy-start(f32[1,64,128]{2,1,0:T(8,128)} %param.9) | copy-start | bytes 98308
  28.4 11.9 %all-to-all-start.1 = ((f32[8,8,128]{2,1,0:T(8,128)}), f32[8,8,128]{2,1,0:T(8,128)S(1)}, u32[]{:S(2)}, u32[]{:S(2)}) async-start(f32[8,8,128]{2,1,0:T(8,128)} %tile.4), calls=%async_computation.1 | async-start | bytes 65536 | tf_op jit(solution)/shard_map/all_to_all | solution.py:148
  39.1 30.8 %collective-permute-start.2 = (bf16[128,1024]{1,0:T(8,128)(2,1)S(1)}, bf16[128,1024]{1,0:T(8,128)(2,1)S(1)}, u32[]{:S(2)}, u32[]{:S(2)}) collective-permute-start(bf16[128,1024]{1,0:T(8,128)(2,1)S(1)} %get-tuple-element.17), channel_id=1, source_target_pairs={{1,0},{3,2},{5,4},{7,6},{9,8},{11,10},{13,12},{15,14},{17,16},{19,... | collective-permute-start | bytes 786440 | tf_op jit(solution)/shard_map/ppermute | solution.py:197
  50.9 18.2 %all-to-all-start.3 = ((f32[16,1,1152]{2,1,0:T(1,128)}), f32[16,1,1152]{2,1,0:T(1,128)S(1)}, u32[]{:S(2)}, u32[]{:S(2)}) async-start(f32[16,1,1152]{2,1,0:T(1,128)} %shard_map.89), calls=%async_computation.3 | async-start | bytes 147456 | tf_op jit(solution)/shard_map/all_to_all | solution.py:148

commit v4 on v3

--- a/solution.py
+++ b/solution.py
@@ -100,22 +100,6 @@
         gq_ref[:, lanes] = dot(flip, (cot * ahead).astype(BF16)).astype(BF16)
 
 
-def settle_kernel(*refs):
-    half = len(refs) // 2
-    for in_ref, out_ref in zip(refs[:half], refs[half:]):
-        out_ref[...] = in_ref[...]
-
-
-def settle(*arrays):
-    size = sum(a.size * a.dtype.itemsize for a in arrays)
-    return pl.pallas_call(
-        settle_kernel,
-        out_shape=tuple(jax.ShapeDtypeStruct(a.shape, a.dtype) for a in arrays),
-        compiler_params=pltpu.CompilerParams(vmem_limit_bytes=VMEM_LIMIT),
-        cost_estimate=pl.CostEstimate(flops=0, bytes_accessed=2 * size, transcendentals=0),
-    )(*[near_in(a) for a in arrays])
-
-
 def pack_kernel(part_ref, squares_ref, packed_ref):
     squares = jnp.sum(squares_ref[...], axis=0, keepdims=True)
     share, taps = part_ref.shape
@@ -125,7 +109,14 @@
         packed_ref[member, :, pl.ds(share * taps, taps)] = squares
 
 
-def clip_kernel(clip_level, packed_ref, grad_ref):
+def clip_kernel(clip_level, by_near, packed_ref, *refs):
+    count = (len(refs) - 2) // 2
+    grad_ref, sems = refs[count], refs[-1]
+    copies = [
+        pltpu.make_async_copy(refs[i], refs[count + 1 + i], sems.at[i]) for i in range(count)
+    ]
+    for copy in copies:
+        copy.start()
     members, _, width = packed_ref.shape
     squares = packed_ref[0, :, pl.ds(width - TAPS, TAPS)]
     for member in range(1, members):
@@ -137,7 +128,9 @@
     for row in range(width // TAPS - 1):
         for member in range(near):
             own = packed_ref[first + member, :, pl.ds(row * TAPS, TAPS)]
-            grad_ref[pl.ds(row * near + member, 1), :] = own * factor
+            grad_ref[pl.ds(row * near + by_near.index(member), 1), :] = own * factor
+    for copy in copies:
+        copy.wait()
 
 
 def near_in(x):
@@ -195,13 +188,10 @@
         ),
     )(filters, near_in(weighted), near_in(ahead), near_in(prod), near_in(behind), near_in(c), near_in(k), near_in(v))
     handed = lax.ppermute(dvalues, "pp", [(1, 0)])
-    (handed,) = settle(handed)
-    grad_q, grad_k = settle(grad_q, grad_k)
-
     near = lax.axis_size(("zl", "core"))
     share = groups_here // near
     cores = lax.axis_size("core")
-    by_near = [zl * cores + core for zl in (1, 2, 0, 3) for core in range(cores)]
+    by_near = [zl * cores + core for zl in (2, 1, 3, 0) for core in range(cores)]
     part = exchange(raw, ("zl", "core"), by_near)
     part = jnp.sum(part.reshape(near, share, TAPS), axis=0)
     wide = lax.axis_size("x")
@@ -220,13 +210,17 @@
         compiler_params=pltpu.CompilerParams(vmem_limit_bytes=VMEM_LIMIT),
     )(near_in(part), near_in(squares))
     halves = reversed(range(lax.axis_size("pp")))
-    packed = exchange(packed, line, [pp * near + i for pp in halves for i in by_near])
+    packed = exchange(packed, line, [pp * near + i for pp in halves for i in range(near)])
     clip_level = 0.25 * math.sqrt(lax.axis_size("pp") * GROUPS * TAPS)
-    grad_f = pl.pallas_call(
-        functools.partial(clip_kernel, clip_level),
-        out_shape=jax.ShapeDtypeStruct((groups_here, TAPS), F32),
-        compiler_params=pltpu.CompilerParams(vmem_limit_bytes=VMEM_LIMIT),
-    )(near_in(packed))
+    whole = jax.ShapeDtypeStruct((length, channels), BF16)
+    grad_f, grad_q, grad_k, handed = pl.pallas_call(
+        functools.partial(clip_kernel, clip_level, by_near),
+        out_shape=(jax.ShapeDtypeStruct((groups_here, TAPS), F32), whole, whole, whole),
+        out_specs=(pl.BlockSpec(memory_space=pltpu.VMEM),)
+        + (pl.BlockSpec(memory_space=pltpu.HBM),) * 3,
+        scratch_shapes=[pltpu.SemaphoreType.DMA((3,))],
+        compiler_params=pltpu.CompilerParams(vmem_limit_bytes=VMEM_LIMIT),
+    )(near_in(packed), near_in(grad_q), near_in(grad_k), near_in(handed))
     return grad_q, grad_k, handed, grad_f
 
 

time: 71.1 us -> 70.2 us (0.987)
  blocking collectives: 16.5 us -> 35.1 us
  starting transfers between devices: 40.4 us -> 25.5 us
  waiting for transfers between devices: 3.12 us -> 0.01 us
  Pallas kernels: 9.12 us -> 7.68 us
    all_to_all x2 -> x3, blocking collectives: 16.5 us -> 35.1 us  [exchange(): lax.all_to_all(rows, axes, 0, 0, tiled=True, axis_index_groups=[order])]
    all_to_all x2 -> x1, starting transfers between devices: 21.7 us -> 6.78 us  [exchange(): lax.all_to_all(rows, axes, 0, 0, tiled=True, axis_index_groups=[order])]
    all_to_all x2 -> x1, waiting for transfers between devices: 3.11 us -> 0.01 us  [exchange(): lax.all_to_all(rows, axes, 0, 0, tiled=True, axis_index_groups=[order])]
    pallas_call x3 -> x1, Pallas kernels: 2.28 us -> 1.52 us  [block(): pl.pallas_call(functools.partial(clip_kernel, clip_level, by_near), out_s...]
  transfers between devices with their start and end apart: 5 -> 4, of which waited for: 1 -> 0; matrix products, arithmetic and copies ran while one was open for 1% -> 1% of each run, Pallas kernels for 10% -> 7%
where the time goes in v4:
time: 70.2 us; the launch traced here: 69.8 us
  blocking collectives  35.1 us (50%)
  starting transfers between devices  25.5 us (36%)
  Pallas kernels  7.68 us (11%)
  between operations  0.75 us (1%)
    all_to_all x3, blocking collectives, exchange(): lax.all_to_all(rows, axes, 0, 0, tiled=True, axis_index_groups=[order])  35.1 us
    ppermute x1, starting transfers between devices, block(): ahead = lax.ppermute(weighted, CTX, [(i + 1, i) for i in range(count - 1)])  11.2 us
    all_to_all x1, starting transfers between devices, exchange(): lax.all_to_all(rows, axes, 0, 0, tiled=True, axis_index_groups=[order])  6.78 us
    ppermute x1, starting transfers between devices, block(): behind = lax.ppermute(prod, CTX, [(i, i + 1) for i in range(count - 1)])  6.29 us
    pallas_call x1, Pallas kernels, block(): pl.pallas_call(mix_kernel, out_shape=(inner, inner, inner), scratch_shape...  3.16 us
    pallas_call x1, Pallas kernels, block(): pl.pallas_call(filter_grad_kernel, out_shape=pltpu.VMEM((groups_here, TAP...  1.52 us
    pallas_call x1, Pallas kernels, block(): pl.pallas_call(functools.partial(clip_kernel, clip_level, by_near), out_s...  1.52 us
    pallas_call x1, Pallas kernels, block(): pl.pallas_call(products_kernel, out_shape=(inner, inner), cost_estimate=p...  1.43 us
  transfers between devices with their start and end apart: 4, of which 0 were waited for; matrix products, arithmetic and copies ran while one was open for 1% of the time, Pallas kernels for 7%

profile of v4, /device:TPU:1, one launch (start us, length us, event | category | flops | bytes accessed | tf_op | source)
XLA Modules:
  0.0 69.8 jit_solution(3293522854273774927)
XLA Ops:
  0.6 1.4 %shard_map.84 = (bf16[128,1024]{1,0:T(8,128)(2,1)S(1)}, bf16[128,1024]{1,0:T(8,128)(2,1)S(1)}) custom-call(bf16[128,1024]{1,0:T(8,128)(2,1)} %bitcast.11, bf16[128,1024]{1,0:T(8,128)(2,1)} %bitcast.13, bf16[128,1024]{1,0:T(8,128)(2,1)} %bitcast.15, bf16[128,1024]{1,0:T(8,128)(2,1)} %bitcast.20), custom_call_target="tpu_custom_call" | custom-call | flops 33554432 | bytes 1572864 | tf_op jit(solution)/shard_map/pallas_call | solution.py:159
  2.1 6.3 %collective-permute-start = (bf16[128,1024]{1,0:T(8,128)(2,1)S(1)}, bf16[128,1024]{1,0:T(8,128)(2,1)S(1)}, u32[]{:S(2)}, u32[]{:S(2)}) collective-permute-start(bf16[128,1024]{1,0:T(8,128)(2,1)S(1)} %get-tuple-element.14.p_ref), channel_id=1, source_target_pairs={{0,16},{16,32},{32,48},{48,64},{64,80},{80,96},{96,112},{112,128},... | collective-permute-start | bytes 786440 | tf_op jit(solution)/shard_map/ppermute | solution.py:168
  8.4 0.0 copy-start
  8.4 0.0 copy-start.1
  8.4 0.0 copy-start.2
  8.4 11.2 %collective-permute-start.1 = (bf16[128,1024]{1,0:T(8,128)(2,1)S(1)}, bf16[128,1024]{1,0:T(8,128)(2,1)S(1)}, u32[]{:S(2)}, u32[]{:S(2)}) collective-permute-start(bf16[128,1024]{1,0:T(8,128)(2,1)S(1)} %get-tuple-element.13.w_ref), channel_id=1, source_target_pairs={{16,0},{32,16},{48,32},{64,48},{80,64},{96,80},{112,96},{128,112},... | collective-permute-start | bytes 786440 | tf_op jit(solution)/shard_map/ppermute | solution.py:169
  19.6 0.0 collective-permute-done.hp_ref
  19.6 1.5 %shard_map.85 = f32[64,128]{1,0:T(8,128)S(1)} custom-call(bf16[128,1024]{1,0:T(8,128)(2,1)S(1)} %get-tuple-element.13.w_ref, bf16[128,1024]{1,0:T(8,128)(2,1)S(1)} %get-tuple-element.14.p_ref, bf16[128,1024]{1,0:T(8,128)(2,1)S(1)} %collective-permute-done.hp_ref), custom_call_target="tpu_custom_call" | custom-call | flops 536870912 | bytes 786432 | tf_op jit(solution)/shard_map/pallas_call | solution.py:171
  21.1 6.7 %all_to_all.28 = f32[8,8,128]{2,1,0:T(8,128)S(1)} all-to-all(f32[8,8,128]{2,1,0:T(8,128)S(1)} %bitcast.17), channel_id=1, replica_groups={{64,80,32,48,96,112,0,16},{65,81,33,49,97,113,1,17},{66,82,34,50,98,114..., dimensions={0} | all-to-all | bytes 65536 | tf_op jit(solution)/shard_map/all_to_all | solution.py:141
  27.8 0.6 tile.4
  28.5 0.0 copy-start.3
  28.5 6.8 %all-to-all-start.1 = ((f32[8,8,128]{2,1,0:T(8,128)}), f32[8,8,128]{2,1,0:T(8,128)S(1)}, u32[]{:S(2)}, u32[]{:S(2)}) async-start(f32[8,8,128]{2,1,0:T(8,128)} %tile.4), calls=%async_computation.1 | async-start | bytes 65536 | tf_op jit(solution)/shard_map/all_to_all | solution.py:141
  35.2 0.0 collective-permute-done.1.hw_ref
  35.2 0.0 copy-done
  35.3 0.0 copy-done.1
  35.3 0.0 copy-done.2
  35.3 0.0 copy-done.3
  35.3 3.2 %shard_map.87 = (bf16[128,1024]{1,0:T(8,128)(2,1)S(1)}, bf16[128,1024]{1,0:T(8,128)(2,1)S(1)}, bf16[128,1024]{1,0:T(8,128)(2,1)S(1)}) custom-call(f32[64,128]{1,0:T(8,128)S(1)} %bitcast.19, bf16[128,1024]{1,0:T(8,128)(2,1)S(1)} %get-tuple-element.13.w_ref, bf16[128,1024]{1,0:T(8,128)(2,1)S(1)} %collective-permute-done.1.hw_ref, ...), custom_call_target="tpu_custom_call" | custom-call | flops 1073741824 | bytes 2621440 | tf_op jit(solution)/shard_map/pallas_call | solution.py:181
  38.5 1.3 %collective-permute-start.2 = (bf16[128,1024]{1,0:T(8,128)(2,1)S(1)}, bf16[128,1024]{1,0:T(8,128)(2,1)S(1)}, u32[]{:S(2)}, u32[]{:S(2)}) collective-permute-start(bf16[128,1024]{1,0:T(8,128)(2,1)S(1)} %get-tuple-element.17), channel_id=1, source_target_pairs={{1,0},{3,2},{5,4},{7,6},{9,8},{11,10},{13,12},{15,14},{17,16},{19,... | collective-permute-start | bytes 786440 | tf_op jit(solution)/shard_map/ppermute | solution.py:190
  39.8 0.0 all-to-all-done.1
  39.8 9.7 %all_to_all.29 = f32[8,1,128]{2,1,0:T(1,128)S(1)} all-to-all(f32[8,1,128]{2,1,0:T(1,128)S(1)} %tile.5), channel_id=1, replica_groups={{8,10,12,14,0,2,4,6},{9,11,13,15,1,3,5,7},{24,26,28,30,16,18,20,22},{25..., dimensions={0} | all-to-all | bytes 8192 | tf_op jit(solution)/shard_map/all_to_all | solution.py:141
  49.6 18.6 %all_to_all.30.packed_ref = f32[16,1,1152]{2,1,0:T(1,128)S(1)} all-to-all(f32[16,1,1152]{2,1,0:T(1,128)S(1)} %shard_map.86), channel_id=1, replica_groups={{1,17,33,49,65,81,97,113,0,16,32,48,64,80,96,112},{3,19,35,51,67,83,99,..., dimensions={0} | all-to-all | bytes 147456 | tf_op jit(solution)/shard_map/all_to_all | solution.py:141
  68.2 0.0 collective-permute-done.2.refs_2_
  68.2 1.5 %shard_map.88 = (f32[64,128]{1,0:T(8,128)}, bf16[128,1024]{1,0:T(8,128)(2,1)}, bf16[128,1024]{1,0:T(8,128)(2,1)}, bf16[128,1024]{1,0:T(8,128)(2,1)}) custom-call(f32[16,1,1152]{2,1,0:T(1,128)S(1)} %all_to_all.30.packed_ref, bf16[128,1024]{1,0:T(8,128)(2,1)S(1)} %get-tuple-element.15.refs_0_, bf16[128,1024]{1,0:T(8,128)(2,1)S(1)} %get-tuple-element.16.refs_1_, ...), custom_call_target="tpu_custom_call" | custom-call | tf_op jit(solution)/shard_map/pallas_call | solution.py:216
  (5 shorter events, 0.1 us)
Async XLA Ops:
  2.1 17.5 %collective-permute-start = (bf16[128,1024]{1,0:T(8,128)(2,1)S(1)}, bf16[128,1024]{1,0:T(8,128)(2,1)S(1)}, u32[]{:S(2)}, u32[]{:S(2)}) collective-permute-start(bf16[128,1024]{1,0:T(8,128)(2,1)S(1)} %get-tuple-element.14.p_ref), channel_id=1, source_target_pairs={{0,16},{16,32},{32,48},{48,64},{64,80},{80,96},{96,112},{112,128},... | collective-permute-start | bytes 786440 | tf_op jit(solution)/shard_map/ppermute | solution.py:168
  8.4 26.9 %copy-start = (bf16[1,128,1024]{2,1,0:T(8,128)(2,1)S(1)}, bf16[1,128,1024]{2,1,0:T(8,128)(2,1)}, u32[]{:S(2)}) copy-start(bf16[1,128,1024]{2,1,0:T(8,128)(2,1)} %param.6) | copy-start | bytes 786436
  8.4 26.9 %copy-start.1 = (bf16[1,128,1024]{2,1,0:T(8,128)(2,1)S(1)}, bf16[1,128,1024]{2,1,0:T(8,128)(2,1)}, u32[]{:S(2)}) copy-start(bf16[1,128,1024]{2,1,0:T(8,128)(2,1)} %param.7) | copy-start | bytes 786436
  8.4 26.9 %copy-start.2 = (bf16[1,128,1024]{2,1,0:T(8,128)(2,1)S(1)}, bf16[1,128,1024]{2,1,0:T(8,128)(2,1)}, u32[]{:S(2)}) copy-start(bf16[1,128,1024]{2,1,0:T(8,128)(2,1)} %param.8) | copy-start | bytes 786436
  8.4 26.8 %collective-permute-start.1 = (bf16[128,1024]{1,0:T(8,128)(2,1)S(1)}, bf16[128,1024]{1,0:T(8,128)(2,1)S(1)}, u32[]{:S(2)}, u32[]{:S(2)}) collective-permute-start(bf16[128,1024]{1,0:T(8,128)(2,1)S(1)} %get-tuple-element.13.w_ref), channel_id=1, source_target_pairs={{16,0},{32,16},{48,32},{64,48},{80,64},{96,80},{112,96},{128,112},... | collective-permute-start | bytes 786440 | tf_op jit(solution)/shard_map/ppermute | solution.py:169
  28.5 6.8 %copy-start.3 = (f32[1,64,128]{2,1,0:T(8,128)S(1)}, f32[1,64,128]{2,1,0:T(8,128)}, u32[]{:S(2)}) copy-start(f32[1,64,128]{2,1,0:T(8,128)} %param.9) | copy-start | bytes 98308
  28.5 11.3 %all-to-all-start.1 = ((f32[8,8,128]{2,1,0:T(8,128)}), f32[8,8,128]{2,1,0:T(8,128)S(1)}, u32[]{:S(2)}, u32[]{:S(2)}) async-start(f32[8,8,128]{2,1,0:T(8,128)} %tile.4), calls=%async_computation.1 | async-start | bytes 65536 | tf_op jit(solution)/shard_map/all_to_all | solution.py:141
  38.5 29.8 %collective-permute-start.2 = (bf16[128,1024]{1,0:T(8,128)(2,1)S(1)}, bf16[128,1024]{1,0:T(8,128)(2,1)S(1)}, u32[]{:S(2)}, u32[]{:S(2)}) collective-permute-start(bf16[128,1024]{1,0:T(8,128)(2,1)S(1)} %get-tuple-element.17), channel_id=1, source_target_pairs={{1,0},{3,2},{5,4},{7,6},{9,8},{11,10},{13,12},{15,14},{17,16},{19,... | collective-permute-start | bytes 786440 | tf_op jit(solution)/shard_map/ppermute | solution.py:190
